TPU v7x, 32 devices: a whole 2x2x4 slice. The times are simulated.
32 devices in a mesh: fold: 2 (over y), vox: 16 (over z, x, core).
Axes of the slice: x: 2, y: 2, z: 4, core: 2. Of those that a mesh axis runs over, the one named last changes fastest.
Arguments:
- volumes: float32 [1024, 12288], P('fold', 'vox'), parts along dimension 0, may hold values from -6 to 6
- record_index: int32 [512], P('fold'), parts along dimension 0, may hold values from 0 to 511
- fold_of: int32 [1024], P('fold'), parts along dimension 0, may hold values from 0 to 4
- held_out: int32 [2], P('fold'), parts along dimension 0, may hold values from 0 to 4
- dictionary: float32 [12288, 512], P('vox'), may hold values from -1 to 1
Outputs:
- new_dictionary: float32 [24576, 512], P(('fold', 'vox')), parts along dimension 0
- code_matrix: float32 [512, 512], P('fold'), parts along dimension 0
- dict_gram: float32 [1024, 512], P('fold'), parts along dimension 0
There are 2 independent parts, one for each index of `fold`. A program takes and returns all parts, laid end to end along the dimension named above; an argument that names none is the same for every part. Nothing has to cross between parts.
All inputs are finite; a program needn't handle non-finite values.
Results may differ from a plain program's by a relative error of at most 0.0001.
Values sent between devices are 32-bit elements; how exact they have to be, the bound alone decides.
A program may use at most 64 MiB of HBM per device.

v0:
```python
import jax
import jax.numpy as jnp
from jax import lax
from jax.sharding import PartitionSpec as P

ISTA_STEPS = 5
penalty = 0.5


def matmul(left, right):
    return jnp.dot(left, right, precision=lax.Precision.HIGHEST, preferred_element_type=jnp.float32)


def inner_cross(left, right):
    return lax.dot_general(
        left,
        right,
        (((0,), (0,)), ((), ())),
        precision=lax.Precision.HIGHEST,
        preferred_element_type=jnp.float32,
    )


def row_bound(matrix):
    return jnp.max(jnp.sum(jnp.abs(matrix), axis=1))


def shrink_codes(correlation, gram_total):
    bound = row_bound(gram_total)
    limit = penalty / bound
    code_rows = jnp.zeros_like(correlation)
    for sweep in range(ISTA_STEPS):
        moved = code_rows - (matmul(code_rows, gram_total) - correlation) / bound
        code_rows = moved - jnp.clip(moved, -limit, limit)
    return code_rows


def shards(volumes, record_index, fold_of, held_out, dictionary):
    batch_rows = volumes[record_index]
    weight = (fold_of[record_index] != held_out[0]).astype(jnp.float32)
    corr_part = matmul(batch_rows, dictionary)
    gram_part = inner_cross(dictionary, dictionary)
    correlation, gram_total = lax.psum((corr_part, gram_part), "vox")
    code_rows = shrink_codes(correlation, gram_total)
    weighted = code_rows * weight[:, None]
    moment = inner_cross(code_rows, weighted)
    target = inner_cross(batch_rows, weighted)
    step_size = 1.0 / (1.0 + row_bound(moment))
    current = dictionary
    stepped = current - step_size * (matmul(current, moment) - target)
    squares = lax.psum(jnp.sum(stepped * stepped, axis=0), "vox")
    current = stepped / jnp.maximum(jnp.sqrt(squares), 1.0)
    stepped = current - step_size * (matmul(current, moment) - target)
    raw_gram = lax.psum(inner_cross(stepped, stepped), "vox")
    divisor = jnp.maximum(jnp.sqrt(jnp.diagonal(raw_gram)), 1.0)
    current = stepped / divisor
    dict_gram = raw_gram / (divisor[:, None] * divisor[None, :])
    return (current, code_rows, dict_gram)


def solution(mesh):
    in_specs = (P("fold", "vox"), P("fold"), P("fold"), P("fold"), P("vox", None))
    out_specs = (P(("fold", "vox"), None), P("fold", None), P("fold", None))
    return jax.shard_map(shards, mesh=mesh, in_specs=in_specs, out_specs=out_specs, check_vma=False)
```

profile of v0, /device:TPU:0, one launch (start us, length us, event | category | flops | bytes accessed | tf_op | source)
XLA Modules:
  0.0 297.6 jit_solution(10499714131739453914)
XLA Ops:
  7.2 0.8 compare_select_fusion
  8.0 5.5 %fusion.42 = f32[512,512]{1,0:T(8,128)} fusion(f32[768,512]{1,0:T(8,128)} %param.9), kind=kOutput, calls=%fused_computation.64 | convolution fusion | flops 2415919104 | bytes 2621440 | tf_op jit(solution)/shard_map/dot_general | solution.py:15
  13.5 2.0 gather_fusion
  15.5 3.4 %fusion.43 = f32[256,512]{1,0:T(8,128)} fusion(f32[256,768]{1,0:T(8,128)} %gather_fusion, f32[768,512]{1,0:T(8,128)S(1)} %copy-done.2), kind=kOutput, calls=%fused_computation.65 | convolution fusion | flops 1207959552 | bytes 2883584 | tf_op jit(solution)/shard_map/dot_general | solution.py:11
  19.0 1.6 copy.14
  20.6 2.1 gather_fusion.1
  23.4 94.5 %all-reduce.6.cloned.1.call-done = (f32[256,512]{1,0:T(8,128)}, f32[512,512]{1,0:T(8,128)}) async-done(((f32[256,512]{1,0:T(8,128)}, f32[512,512]{1,0:T(8,128)}), (f32[256,512]{1,0:T(8,128)}, f32[512,512]{1,0:T(8,128)})) %all-reduce.6.cloned.1.call-update) | async-done | bytes 1572880 | tf_op jit(solution)/shard_map/psum | solution.py:43
  117.9 1.4 abs_reduce_fusion.1
  119.9 3.8 %fusion.4 = f32[256,512]{1,0:T(8,128)} fusion(f32[256,512]{1,0:T(8,128)} %get-tuple-element.9, f32[512,512]{1,0:T(8,128)} %get-tuple-element.10, f32[]{:T(128)} %reduce_max.18), kind=kOutput, calls=%fused_computation.15 | convolution fusion | flops 805699584 | bytes 2097156 | tf_op jit(solution)/shard_map/dot_general | solution.py:11
  124.4 3.6 %fusion.6 = f32[256,512]{1,0:T(8,128)S(1)} fusion(f32[256,512]{1,0:T(8,128)} %get-tuple-element.9, f32[512,512]{1,0:T(8,128)} %get-tuple-element.10, f32[256,512]{1,0:T(8,128)} %fusion.4, f32[]{:T(128)S(6)} %neg.2, f32[]{:T(128)S(6)} %div.49, f32[]{:T(128)} %reduce_max.18), kind=kOutput, calls=%fused_computation.17 | convolution fusion | flops 806486016 | bytes 2621452 | tf_op jit(solution)/shard_map/dot_general | solution.py:11
  128.0 1.8 fusion.8
  129.8 1.8 fusion.10
  131.6 1.9 minimum_subtract_fusion
  133.5 2.7 fusion.14
  136.2 2.1 abs_reduce_fusion
  139.6 6.2 %multiply_reduce_fusion = (f32[512]{0:T(512)S(1)}, f32[768,512]{0,1:T(8,128)}) fusion(f32[768,512]{0,1:T(8,128)} %copy.14, f32[768,512]{0,1:T(8,128)} %fusion.14, f32[512,512]{0,1:T(8,128)} %get-tuple-element.12, f32[768,512]{1,0:T(8,128)S(1)} %copy-done.2, f32[]{:T(128)S(6)} %div.54), kind=kOutput, calls=%fused_computation.7 | convolution fusion | flops 2417884672 | bytes 7342084 | tf_op jit(solution)/shard_map/dot_general | solution.py:11
  145.7 30.2 %psum.30 = f32[512]{0:T(512)S(1)} all-reduce(f32[512]{0:T(512)S(1)} %get-tuple-element.13), channel_id=1, replica_groups=mesh['fold'=2,'vox'=16] {'vox'}, use_global_device_ids=true, to_apply=%region_7.8 | all-reduce | flops 512 | bytes 4096 | tf_op jit(solution)/shard_map/psum | solution.py:51
  175.9 5.7 %multiply_subtract_fusion = f32[768,512]{0,1:T(8,128)S(1)} fusion(f32[768,512]{0,1:T(8,128)} %fusion.14, f32[512,512]{0,1:T(8,128)} %get-tuple-element.12, f32[768,512]{0,1:T(8,128)} %get-tuple-element.14, f32[512]{0:T(512)S(1)} %sqrt_maximum_fusion.1, f32[]{:T(128)S(6)} %div.54), kind=kOutput, calls=%fused_computation.6 | convolution fusion | flops 2417885184 | bytes 5769220 | tf_op jit(solution)/shard_map/dot_general | solution.py:11
  181.6 3.7 %fusion.44 = f32[512,512]{1,0:T(8,128)} fusion(f32[768,512]{0,1:T(8,128)S(1)} %multiply_subtract_fusion), kind=kOutput, calls=%fused_computation.66 | convolution fusion | flops 2415919104 | bytes 2621440 | tf_op jit(solution)/shard_map/dot_general | solution.py:15
  185.3 91.0 %all-reduce.4.cloned.1.call-done = f32[512,512]{1,0:T(8,128)} async-done(((f32[512,512]{1,0:T(8,128)}), f32[512,512]{1,0:T(8,128)}) %all-reduce.4.cloned.1.call-update) | async-done | bytes 1048592 | tf_op jit(solution)/shard_map/psum | solution.py:54
  276.4 8.7 %gather_fusion.2 = f32[512]{0:T(512)S(1)} fusion(f32[512,512]{1,0:T(8,128)} %all-reduce.4.cloned.1.call-done, s32[512]{0:T(512)S(1)} %bitcast.25), kind=kCustom, calls=%fused_computation.2 | custom fusion | bytes 8192 | tf_op jit(solution)/shard_map/jit(diagonal)/cond/branch_0_fun/gather | solution.py:55
  285.1 1.3 broadcast_divide_fusion
  286.5 3.1 %copy.17 = f32[768,512]{1,0:T(8,128)} copy(f32[768,512]{0,1:T(8,128)} %broadcast_divide_fusion) | data formatting | bytes 3145728
  289.6 1.2 multiply_divide_fusion
  (27 shorter events, 1.4 us)
Async XLA Ops:
  7.2 6.4 %copy-start = (f32[512,768]{1,0:T(8,128)S(1)}, f32[512,768]{1,0:T(8,128)}, u32[]{:S(2)}) copy-start(f32[512,768]{1,0:T(8,128)} %param.5) | copy-start | bytes 4718596
  7.2 110.7 %all-reduce.6.cloned.1.call-start = ((), (), s32[]{:S(2)}) async-start(), calls=%async_computation.1 | async-start | bytes 3145728 | tf_op jit(solution)/shard_map/psum | solution.py:43
  13.5 2.0 copy-start.2
  19.0 1.7 copy-start.1
  19.0 257.4 %all-reduce.4.cloned.1.call-start = ((), (), s32[]{:S(2)}) async-start(), calls=%async_computation | async-start | bytes 2097152 | tf_op jit(solution)/shard_map/psum | solution.py:54
  124.4 3.6 %copy-start.6 = (f32[512,512]{1,0:T(8,128)S(1)}, f32[512,512]{1,0:T(8,128)}, u32[]{:S(2)}) copy-start(f32[512,512]{1,0:T(8,128)} %get-tuple-element.10) | copy-start | bytes 3145732
  124.4 3.6 %copy-start.7 = (f32[256,512]{1,0:T(8,128)S(1)}, f32[256,512]{1,0:T(8,128)}, u32[]{:S(2)}) copy-start(f32[256,512]{1,0:T(8,128)} %get-tuple-element.9) | copy-start | bytes 1572868
  131.6 1.9 copy-start.4
  133.5 4.8 %copy-start.5 = (f32[256,512]{1,0:T(8,128)}, f32[256,512]{1,0:T(8,128)S(1)}, u32[]{:S(2)}) copy-start(f32[256,512]{1,0:T(8,128)S(1)} %minimum_subtract_fusion) | copy-start | bytes 1572868
  286.5 3.1 %copy-start.3 = (f32[512,512]{1,0:T(8,128)S(1)}, f32[512,512]{1,0:T(8,128)}, u32[]{:S(2)}) copy-start(f32[512,512]{1,0:T(8,128)} %all-reduce.4.cloned.1.call-done) | copy-start | bytes 3145732
Sparse Core Ops, SparseCore 0:
  19.1 98.7 all-reduce.5
  185.4 90.8 all-reduce.3
where the time goes:
time: 298 us
  waiting for transfers between devices  186 us (62%)
  matrix products  42.1 us (14%)
  blocking collectives  30.2 us (10%)
  local copies, waits for them, and re-layouts  17.6 us (6%)
  between operations  16.2 us (5%)
  other arithmetic  5.95 us (2%)
    psum x1, waiting for transfers between devices, shards(): correlation, gram_total = lax.psum((corr_part, gram_part), 'vox')  94.5 us
    psum x1, waiting for transfers between devices, shards(): raw_gram = lax.psum(inner_cross(stepped, stepped), 'vox')  91 us
    psum x1, blocking collectives, shards(): squares = lax.psum(jnp.sum(stepped * stepped, axis=0), 'vox')  30.2 us
    dot_general x8, matrix products, matmul(): jnp.dot(left, right, precision=lax.Precision.HIGHEST, preferred_element_t...  28.1 us
    dot_general x4, matrix products, inner_cross(): lax.dot_general(left, right, (((0,), (0,)), ((), ())), precision=lax.Prec...  13.9 us
    gather x1, local copies, waits for them, and re-layouts, shards(): divisor = jnp.maximum(jnp.sqrt(jnp.diagonal(raw_gram)), 1.0)  8.74 us
  transfers between devices with their start and end apart: 2, of which 2 were waited for; matrix products, arithmetic and copies ran while one was open for 1% of the time, Pallas kernels for 0%

commit v1 on v0

--- a/solution.py
+++ b/solution.py
@@ -48,7 +48,7 @@
     step_size = 1.0 / (1.0 + row_bound(moment))
     current = dictionary
     stepped = current - step_size * (matmul(current, moment) - target)
-    squares = lax.psum(jnp.sum(stepped * stepped, axis=0), "vox")
+    squares = jnp.sum(lax.all_gather(jnp.sum(stepped * stepped, axis=0), "vox"), axis=0)
     current = stepped / jnp.maximum(jnp.sqrt(squares), 1.0)
     stepped = current - step_size * (matmul(current, moment) - target)
     raw_gram = lax.psum(inner_cross(stepped, stepped), "vox")

time: 298 us -> 288 us (0.966)
  blocking collectives: 30.2 us -> 19.5 us
    psum x1 -> x0, blocking collectives: 30.2 us -> none  [shards(): squares = lax.psum(jnp.sum(stepped * stepped, axis=0), 'vox')]
    all_gather x0 -> x1, blocking collectives: none -> 19.5 us  [shards(): lax.all_gather(jnp.sum(stepped * stepped, axis=0), 'vox')]
where the time goes in v1:
time: 288 us; the launch traced here: 287 us
  waiting for transfers between devices  186 us (65%)
  matrix products  42.1 us (15%)
  blocking collectives  19.5 us (7%)
  local copies, waits for them, and re-layouts  17.6 us (6%)
  between operations  16.2 us (6%)
  other arithmetic  5.99 us (2%)
    psum x1, waiting for transfers between devices, shards(): correlation, gram_total = lax.psum((corr_part, gram_part), 'vox')  94.5 us
    psum x1, waiting for transfers between devices, shards(): raw_gram = lax.psum(inner_cross(stepped, stepped), 'vox')  91 us
    dot_general x8, matrix products, matmul(): jnp.dot(left, right, precision=lax.Precision.HIGHEST, preferred_element_t...  28.1 us
    all_gather x1, blocking collectives, shards(): lax.all_gather(jnp.sum(stepped * stepped, axis=0), 'vox')  19.5 us
    dot_general x4, matrix products, inner_cross(): lax.dot_general(left, right, (((0,), (0,)), ((), ())), precision=lax.Prec...  13.9 us
    gather x1, local copies, waits for them, and re-layouts, shards(): divisor = jnp.maximum(jnp.sqrt(jnp.diagonal(raw_gram)), 1.0)  8.74 us
  transfers between devices with their start and end apart: 2, of which 2 were waited for; matrix products, arithmetic and copies ran while one was open for 1% of the time, Pallas kernels for 0%

profile of v1, /device:TPU:0, one launch (start us, length us, event | category | flops | bytes accessed | tf_op | source)
XLA Modules:
  0.0 287.0 jit_solution(2772708440266581798)
XLA Ops:
  7.2 0.8 compare_select_fusion
  8.0 5.5 %fusion.42 = f32[512,512]{1,0:T(8,128)} fusion(f32[768,512]{1,0:T(8,128)} %param.9), kind=kOutput, calls=%fused_computation.64 | convolution fusion | flops 2415919104 | bytes 2621440 | tf_op jit(solution)/shard_map/dot_general | solution.py:15
  13.5 2.0 gather_fusion
  15.5 3.4 %fusion.43 = f32[256,512]{1,0:T(8,128)} fusion(f32[256,768]{1,0:T(8,128)} %gather_fusion, f32[768,512]{1,0:T(8,128)S(1)} %copy-done.2), kind=kOutput, calls=%fused_computation.65 | convolution fusion | flops 1207959552 | bytes 2883584 | tf_op jit(solution)/shard_map/dot_general | solution.py:11
  19.0 1.6 copy.19
  20.6 2.1 gather_fusion.1
  23.4 94.5 %all-reduce.6.cloned.1.call-done = (f32[256,512]{1,0:T(8,128)}, f32[512,512]{1,0:T(8,128)}) async-done(((f32[256,512]{1,0:T(8,128)}, f32[512,512]{1,0:T(8,128)}), (f32[256,512]{1,0:T(8,128)}, f32[512,512]{1,0:T(8,128)})) %all-reduce.6.cloned.1.call-update) | async-done | bytes 1572880 | tf_op jit(solution)/shard_map/psum | solution.py:43
  117.9 1.4 abs_reduce_fusion.1
  119.9 3.8 %fusion.4 = f32[256,512]{1,0:T(8,128)} fusion(f32[256,512]{1,0:T(8,128)} %get-tuple-element.12, f32[512,512]{1,0:T(8,128)} %get-tuple-element.13, f32[]{:T(128)} %reduce_max.18), kind=kOutput, calls=%fused_computation.15 | convolution fusion | flops 805699584 | bytes 2097156 | tf_op jit(solution)/shard_map/dot_general | solution.py:11
  124.4 3.6 %fusion.6 = f32[256,512]{1,0:T(8,128)S(1)} fusion(f32[256,512]{1,0:T(8,128)} %get-tuple-element.12, f32[512,512]{1,0:T(8,128)} %get-tuple-element.13, f32[256,512]{1,0:T(8,128)} %fusion.4, f32[]{:T(128)S(6)} %neg.2, f32[]{:T(128)S(6)} %div.49, f32[]{:T(128)} %reduce_max.18), kind=kOutput, calls=%fused_computation.17 | convolution fusion | flops 806486016 | bytes 2621452 | tf_op jit(solution)/shard_map/dot_general | solution.py:11
  128.0 1.8 fusion.8
  129.8 1.8 fusion.10
  131.6 1.9 minimum_subtract_fusion
  133.5 2.7 fusion.14
  136.2 2.1 abs_reduce_fusion
  139.6 6.2 %multiply_reduce_fusion = (f32[512]{0:T(512)S(1)}, f32[768,512]{0,1:T(8,128)}) fusion(f32[768,512]{0,1:T(8,128)} %copy.19, f32[768,512]{0,1:T(8,128)} %fusion.14, f32[512,512]{0,1:T(8,128)} %get-tuple-element.15, f32[768,512]{1,0:T(8,128)S(1)} %copy-done.2, f32[]{:T(128)S(6)} %div.54), kind=kOutput, calls=%fused_computation.7 | convolution fusion | flops 2417884672 | bytes 7342084 | tf_op jit(solution)/shard_map/dot_general | solution.py:11
  145.7 19.5 %all-gather.1 = f32[16,1,512]{2,1,0:T(1,128)S(1)} all-gather(f32[1,1,512]{2,1,0:T(1,128)S(1)} %bitcast.27), channel_id=2, replica_groups=mesh['fold'=2,'vox'=16] {'vox'}, dimensions={0}, use_global_device_ids=true | all-gather | bytes 34816 | tf_op jit(solution)/shard_map/all_gather | solution.py:51
  165.3 5.7 %multiply_subtract_fusion = f32[768,512]{0,1:T(8,128)S(1)} fusion(f32[768,512]{0,1:T(8,128)} %fusion.14, f32[512,512]{0,1:T(8,128)} %get-tuple-element.15, f32[768,512]{0,1:T(8,128)} %get-tuple-element.17, f32[512]{0:T(512)S(1)} %sqrt_maximum_fusion.1, f32[]{:T(128)S(6)} %div.54), kind=kOutput, calls=%fused_computation.6 | convolution fusion | flops 2417885184 | bytes 5769220 | tf_op jit(solution)/shard_map/dot_general | solution.py:11
  171.1 3.7 %fusion.44 = f32[512,512]{1,0:T(8,128)} fusion(f32[768,512]{0,1:T(8,128)S(1)} %multiply_subtract_fusion), kind=kOutput, calls=%fused_computation.66 | convolution fusion | flops 2415919104 | bytes 2621440 | tf_op jit(solution)/shard_map/dot_general | solution.py:15
  174.8 91.0 %all-reduce.4.cloned.1.call-done = f32[512,512]{1,0:T(8,128)} async-done(((f32[512,512]{1,0:T(8,128)}), f32[512,512]{1,0:T(8,128)}) %all-reduce.4.cloned.1.call-update) | async-done | bytes 1048592 | tf_op jit(solution)/shard_map/psum | solution.py:54
  265.8 8.7 %gather_fusion.2 = f32[512]{0:T(512)S(1)} fusion(f32[512,512]{1,0:T(8,128)} %all-reduce.4.cloned.1.call-done, s32[512]{0:T(512)S(1)} %bitcast.26), kind=kCustom, calls=%fused_computation.2 | custom fusion | bytes 8192 | tf_op jit(solution)/shard_map/jit(diagonal)/cond/branch_0_fun/gather | solution.py:55
  274.5 1.3 broadcast_divide_fusion
  275.9 3.1 %copy.22 = f32[768,512]{1,0:T(8,128)} copy(f32[768,512]{0,1:T(8,128)} %broadcast_divide_fusion) | data formatting | bytes 3145728
  279.0 1.2 multiply_divide_fusion
  (28 shorter events, 1.5 us)
Async XLA Ops:
  7.2 6.4 %copy-start = (f32[512,768]{1,0:T(8,128)S(1)}, f32[512,768]{1,0:T(8,128)}, u32[]{:S(2)}) copy-start(f32[512,768]{1,0:T(8,128)} %param.5) | copy-start | bytes 4718596
  7.2 110.7 %all-reduce.6.cloned.1.call-start = ((), (), s32[]{:S(2)}) async-start(), calls=%async_computation.1 | async-start | bytes 3145728 | tf_op jit(solution)/shard_map/psum | solution.py:43
  13.5 2.0 copy-start.2
  19.0 1.7 copy-start.1
  19.0 246.8 %all-reduce.4.cloned.1.call-start = ((), (), s32[]{:S(2)}) async-start(), calls=%async_computation | async-start | bytes 2097152 | tf_op jit(solution)/shard_map/psum | solution.py:54
  124.4 3.6 %copy-start.6 = (f32[512,512]{1,0:T(8,128)S(1)}, f32[512,512]{1,0:T(8,128)}, u32[]{:S(2)}) copy-start(f32[512,512]{1,0:T(8,128)} %get-tuple-element.13) | copy-start | bytes 3145732
  124.4 3.6 %copy-start.7 = (f32[256,512]{1,0:T(8,128)S(1)}, f32[256,512]{1,0:T(8,128)}, u32[]{:S(2)}) copy-start(f32[256,512]{1,0:T(8,128)} %get-tuple-element.12) | copy-start | bytes 1572868
  131.6 1.9 copy-start.4
  133.5 4.8 %copy-start.5 = (f32[256,512]{1,0:T(8,128)}, f32[256,512]{1,0:T(8,128)S(1)}, u32[]{:S(2)}) copy-start(f32[256,512]{1,0:T(8,128)S(1)} %minimum_subtract_fusion) | copy-start | bytes 1572868
  275.9 3.1 %copy-start.3 = (f32[512,512]{1,0:T(8,128)S(1)}, f32[512,512]{1,0:T(8,128)}, u32[]{:S(2)}) copy-start(f32[512,512]{1,0:T(8,128)} %all-reduce.4.cloned.1.call-done) | copy-start | bytes 3145732
Sparse Core Ops, SparseCore 0:
  19.1 98.7 all-reduce.5
  174.9 90.8 all-reduce.3
